TPU v7x, 32 devices: a whole 2x2x4 slice. The times are simulated.
32 devices in a mesh: groups: 2 (over y), fsdp: 8 (over z, core), band: 2 (over x).
Axes of the slice: x: 2, y: 2, z: 4, core: 2. Of those that a mesh axis runs over, the one named last changes fastest.
Arguments:
- hidden_in: bfloat16 [16, 4, 64, 5632], P(('groups', 'fsdp'), 'band'), parts along dimension 0, may hold values from -6 to 6
- tap_weights: bfloat16 [9, 5632], P(None, 'fsdp'), may hold values from -2 to 2
- tap_bias: bfloat16 [5632], P('fsdp'), may hold values from -3 to 3
- w_out: bfloat16 [2816, 2240], P('fsdp'), may hold values from -0.109375 to 0.109375
- cotangent: bfloat16 [16, 4, 64, 2240], P(('groups', 'fsdp'), 'band'), parts along dimension 0, may hold values from -0.59765625 to 0.59765625
Outputs:
- block_out: bfloat16 [16, 4, 64, 2240], P(('groups', 'fsdp'), 'band'), parts along dimension 0
- d_hidden: bfloat16 [16, 4, 64, 5632], P(('groups', 'fsdp'), 'band'), parts along dimension 0
- d_taps: float32 [18, 5632], P('groups', 'fsdp'), parts along dimension 0
- d_tap_bias: float32 [11264], P(('groups', 'fsdp')), parts along dimension 0
There are 2 independent parts, one for each index of `groups`. A program takes and returns all parts, laid end to end along the dimension named above; an argument that names none is the same for every part. Nothing has to cross between parts.
All inputs are finite; a program needn't handle non-finite values.
Results may differ from a plain program's by a relative error of at most 0.0049.
Values may be sent and summed in bfloat16 or wider, within the bound.
No kernel may reach another device: no remote copies, remote signals or barrier semaphores. Data moves between devices by JAX's collectives and lax.ppermute only.
A program may use at most 128 MiB of HBM per device.

v0:
```python
import jax
import jax.numpy as jnp
from jax import lax
from jax.sharding import PartitionSpec as P


def with_halo(cells, sides, width):
    for axis, dim in sides:
        count = lax.axis_size(axis)
        ends = count - 1
        head = lax.slice_in_dim(cells, 0, width, axis=dim)
        tail = lax.slice_in_dim(cells, cells.shape[dim] - width, cells.shape[dim], axis=dim)
        cells = jnp.concatenate(
            [
                lax.ppermute(tail, axis, [(i, (i + 1) % count) for i in range(ends)]),
                cells,
                lax.ppermute(head, axis, [((i + 1) % count, i) for i in range(ends)]),
            ],
            axis=dim,
        )
    return cells


def body(hidden_in, tap_weights, tap_bias, w_out, cotangent):
    kernel_all, offset_all = (
        lax.all_gather(tap_weights, "fsdp", axis=1, tiled=True),
        lax.all_gather(tap_bias, "fsdp", axis=0, tiled=True),
    )
    kernel = kernel_all.astype(jnp.float32)
    offset = offset_all.astype(jnp.float32)
    image_count, row_count, col_count, channels = hidden_in.shape
    hidden_units = channels // 2
    token_count = image_count * row_count * col_count
    extended = with_halo(hidden_in, (("band", 1),), 1)
    padded = jnp.pad(extended, ((0, 0), (0, 0), (1, 1), (0, 0)))
    summed = jnp.zeros((image_count, row_count, col_count, channels), jnp.float32) + offset
    for tap_row in range(3):
        for tap_col in range(3):
            window = padded[:, tap_row : tap_row + row_count, tap_col : tap_col + col_count, :]
            summed = summed + kernel[3 * tap_row + tap_col] * window
    values_half = summed[..., :hidden_units]
    gate_half = summed[..., hidden_units:]
    sigmoid_gate = jax.nn.sigmoid(gate_half)
    silu_gate = gate_half * sigmoid_gate
    glu_flat = (values_half * silu_gate).astype(jnp.bfloat16).reshape(token_count, hidden_units)
    grad_flat = cotangent.reshape(token_count, cotangent.shape[3])
    features = grad_flat.shape[1]
    piece = lax.all_gather(w_out, "fsdp", axis=0, tiled=True)
    out_sum = jnp.dot(glu_flat, piece, preferred_element_type=jnp.float32)
    d_piece = lax.dot_general(
        grad_flat, piece, (((1,), (1,)), ((), ())), preferred_element_type=jnp.float32
    )
    out_sum, d_glu = (out_sum, d_piece)
    block_out = out_sum.astype(jnp.bfloat16).reshape(image_count, row_count, col_count, features)
    d_glu = d_glu.reshape(image_count, row_count, col_count, hidden_units)
    slope = sigmoid_gate * (1.0 + gate_half * (1.0 - sigmoid_gate))
    d_pre = jnp.concatenate([d_glu * silu_gate, d_glu * values_half * slope], axis=-1).astype(
        jnp.bfloat16
    )
    d_extended = with_halo(d_pre, (("band", 1),), 1)
    d_pad = jnp.pad(d_extended, ((0, 0), (0, 0), (1, 1), (0, 0)))
    d_image = jnp.zeros((image_count, row_count, col_count, channels), jnp.float32)
    tap_terms = []
    for tap_row in range(3):
        for tap_col in range(3):
            d_window = d_pad[
                :, 2 - tap_row : 2 - tap_row + row_count, 2 - tap_col : 2 - tap_col + col_count, :
            ]
            d_image = d_image + kernel[3 * tap_row + tap_col] * d_window
            window = padded[:, tap_row : tap_row + row_count, tap_col : tap_col + col_count, :]
            tap_terms.append(
                jnp.einsum("srck,srck->k", window, d_pre, preferred_element_type=jnp.float32)
            )
    d_hidden = d_image.astype(jnp.bfloat16)
    tap_grad = jnp.stack(tap_terms)
    bias_grad = jnp.sum(d_pre.astype(jnp.float32), axis=(0, 1, 2))
    tap_grad, bias_grad = lax.psum((tap_grad, bias_grad), "band")
    tap_share, bias_share = (
        lax.psum_scatter(tap_grad, "fsdp", scatter_dimension=1, tiled=True),
        lax.psum_scatter(bias_grad, "fsdp", scatter_dimension=0, tiled=True),
    )
    return (block_out, d_hidden, tap_share, bias_share)


def solution(mesh):
    placed = (
        P(("groups", "fsdp"), "band", None, None),
        P(None, "fsdp"),
        P("fsdp"),
        P("fsdp", None),
        P(("groups", "fsdp"), "band", None, None),
    )
    return jax.shard_map(
        body,
        mesh=mesh,
        in_specs=placed,
        out_specs=(
            P(("groups", "fsdp"), "band", None, None),
            P(("groups", "fsdp"), "band", None, None),
            P("groups", "fsdp"),
            P(("groups", "fsdp")),
        ),
        check_vma=False,
    )
```

profile of v0, /device:TPU:0, one launch (start us, length us, event | category | flops | bytes accessed | tf_op | source)
XLA Modules:
  0.0 235.5 jit_solution(369298379283991862)
XLA Ops:
  7.2 0.0 copy-start
  7.2 0.0 copy-start.22
  7.2 0.0 all-gather.3.cloned.1.call-start
  7.3 0.7 all-gather.3.cloned.1.call-update
  8.0 0.0 reduce-scatter.4.cloned.1.call-start
  8.0 2.6 %fusion.26 = (bf16[1,1,64,5632]{3,2,1,0:T(8,128)(2,1)}, bf16[1,1,64,5632]{3,2,1,0:T(8,128)(2,1)}) fusion(bf16[1,2,64,5632]{3,2,1,0:T(8,128)(2,1)} %param.5), kind=kLoop, calls=%fused_computation.70 | loop fusion | bytes 2883584 | tf_op jit(solution)/shard_map/slice | solution.py:11
  10.6 1.3 collective-permute-start.1
  11.9 5.0 %collective-permute-start = (bf16[1,1,64,5632]{3,2,1,0:T(8,128)(2,1)}, bf16[1,1,64,5632]{3,2,1,0:T(8,128)(2,1)S(1)}, u32[]{:S(2)}, u32[]{:S(2)}) collective-permute-start(bf16[1,1,64,5632]{3,2,1,0:T(8,128)(2,1)} %get-tuple-element.40), channel_id=1, source_target_pairs={{0,1},{2,3},{4,5},{6,7},{8,9},{10,11},{12,13},{14,15},{16,17},{18,... | collective-permute-start | bytes 2162696 | tf_op jit(solution)/shard_map/ppermute | solution.py:15
  16.9 0.6 fusion.27
  18.1 0.2 dynamic-update-slice
  18.4 31.5 %all-reduce.2 = bf16[5632]{0:T(1024)(128)(2,1)S(1)} all-reduce(bf16[5632]{0:T(1024)(128)(2,1)S(1)} %dynamic-update-slice), channel_id=1, replica_groups=mesh['groups'=2,'fsdp'=8,'band'=2] {'fsdp'}, use_global_device_ids=true, to_apply=%add.2 | all-reduce | flops 5632 | bytes 22528
  49.8 0.6 convert_element_type.109
  50.5 25.0 %all-gather = bf16[8,704,9]{1,2,0:T(8,128)(2,1)S(1)} all-gather(bf16[1,704,9]{1,2,0:T(8,128)(2,1)S(1)} %bitcast.101), channel_id=1, replica_groups=mesh['groups'=2,'fsdp'=8,'band'=2] {'fsdp'}, dimensions={0}, use_global_device_ids=true | all-gather | bytes 114048 | tf_op jit(solution)/shard_map/all_gather | solution.py:26
  75.5 0.7 copy_convert_fusion
  76.2 1.8 reshape.190
  78.7 2.4 %slice_reduce_fusion.8 = (f32[5632]{0:T(1024)S(1)}, f32[5632]{0:T(1024)S(1)}, f32[5632]{0:T(1024)S(1)}, f32[5632]{0:T(1024)S(1)}, f32[5632]{0:T(1024)S(1)}, /*in...) fusion(f32[9,5632]{1,0:T(8,128)} %bitcast.97), kind=kLoop, calls=%fused_computation.69 | loop fusion | bytes 405504 | tf_op jit(solution)/shard_map/slice | solution.py:40
  81.2 1.1 select_maximum_fusion.3
  82.3 1.6 copy-done.1
  83.9 3.9 %multiply_add_fusion = f32[1,2,64,5632]{3,2,1,0:T(8,128)} fusion(bf16[1,2,64,5632]{3,2,1,0:T(8,128)(2,1)S(1)} %copy-done.3, f32[5632]{0:T(1024)S(1)} %get-tuple-element.18, f32[5632]{0:T(1024)S(1)} %get-tuple-element.19, f32[5632]{0:T(1024)S(1)} %get-tuple-element.20, f32[5632]{0:T(1024)S(1)} %get-tuple-element.21, f32[5632]{0:T(1024)S(1)} %get-tuple-element.22, ...), kind=kLoop, calls=%fused_computation.39 | loop fusion | flops 20905984 | bytes 14643200 | tf_op jit(solution)/shard_map/add | solution.py:40
  87.8 46.5 %all-gather.3.cloned.1.call-done = bf16[2816,2240]{1,0:T(8,128)(2,1)} async-done(((bf16[352,2240]{1,0:T(8,128)(2,1)}), bf16[2816,2240]{1,0:T(8,128)(2,1)}) %all-gather.3.cloned.1.call-update) | async-done | bytes 12615696 | tf_op jit(solution)/shard_map/all_gather | solution.py:48
  134.3 10.8 %multiply_convert_fusion = (bf16[1,2,64,2816]{3,2,1,0:T(8,128)(2,1)S(1)}, bf16[1,2,64,2816]{3,2,1,0:T(8,128)(2,1)S(1)}, bf16[1,2,64,2816]{3,2,1,0:T(8,128)(2,1)}) fusion(f32[1,2,64,5632]{3,2,1,0:T(8,128)} %multiply_add_fusion, bf16[2816,2240]{1,0:T(8,128)(2,1)} %all-gather.3.cloned.1.call-done, bf16[1,2,64,2240]{3,2,1,0:T(8,128)(2,1)S(1)} %copy-done), kind=kOutput, calls=%fused_computation.52 | convolution fusion | flops 1620213760 | bytes 18235392 | tf_op jit(solution)/shard_map/dot_general | solution.py:50
  145.1 1.2 fusion.23
  146.3 0.2 copy-done.5
  146.5 0.5 copy-done.7
  147.0 3.8 %fusion.19 = (f32[5632]{0:T(1024)S(1)}, f32[5632]{0:T(1024)S(1)}, f32[5632]{0:T(1024)S(1)}, f32[5632]{0:T(1024)S(1)}, f32[5632]{0:T(1024)S(1)}, /*index=5*/f32[5...) fusion(bf16[1,1,64,5632]{3,2,1,0:T(8,128)(2,1)S(1)} %copy-done.5, ...), kind=kLoop, calls=%fused_computation.36 | loop fusion | flops 28785152 | bytes 13178880 | tf_op jit(solution)/shard_map/srck,srck->k/dot_general | solution.py:72
  150.8 0.6 stack.37
  151.4 0.6 stack.31
  152.0 0.6 stack.34
  152.7 0.6 stack.30
  153.3 0.6 stack.32
  153.9 0.6 stack.33
  154.5 0.6 stack.35
  155.2 0.6 stack.36
  155.8 0.6 stack.38
  156.4 3.3 %collective-permute-start.2 = (bf16[1,1,64,5632]{3,2,1,0:T(8,128)(2,1)}, bf16[1,1,64,5632]{3,2,1,0:T(8,128)(2,1)S(1)}, u32[]{:S(2)}, u32[]{:S(2)}) collective-permute-start(bf16[1,1,64,5632]{3,2,1,0:T(8,128)(2,1)} %get-tuple-element.37), channel_id=1, source_target_pairs={{0,1},{2,3},{4,5},{6,7},{8,9},{10,11},{12,13},{14,15},{16,17},{18,... | collective-permute-start | bytes 2162696 | tf_op jit(solution)/shard_map/ppermute | solution.py:15
  159.7 1.5 collective-permute-start.3
  161.2 3.2 %stack.39 = f32[9,5632]{1,0:T(8,128)} concatenate(f32[1,5632]{1,0:T(1,128)} %stack.30, f32[1,5632]{1,0:T(1,128)} %stack.31, f32[1,5632]{1,0:T(1,128)} %stack.32, f32[1,5632]{1,0:T(1,128)} %stack.33, f32[1,5632]{1,0:T(1,128)} %stack.34, f32[1,5632]{1,0:T(1,128)} %stack.35, f32[1,5632]{1,0:T(1,128)} %stack.36, f32[1,5632]{1,0:T(1,128)} %stack.37, f32[1,5632]{1,0:T(1,128)} %stack.38), dimensions={0} | concatenate | bytes 405504 | tf_op jit(solution)/shard_map/stack | solution.py:75
  164.4 3.0 %copy.79 = f32[9,5632]{0,1:T(8,128)} copy(f32[9,5632]{1,0:T(8,128)} %stack.39) | data formatting | bytes 405504
  167.3 0.0 reduce-scatter.4.cloned.1.call-update
  167.3 10.8 %convolution_convert_fusion = bf16[128,2240]{0,1:T(8,128)(2,1)} fusion(bf16[128,2816]{1,0:T(8,128)(2,1)} %bitcast.98, bf16[2816,2240]{1,0:T(8,128)(2,1)} %all-gather.3.cloned.1.call-done), kind=kOutput, calls=%fused_computation.15 | convolution fusion | flops 1615093760 | bytes 13910016 | tf_op jit(solution)/shard_map/dot_general | solution.py:49
  178.2 2.1 copy.15
  180.3 0.8 convert_reduce_fusion
  181.1 27.7 %all-reduce.3 = f32[5632]{0:T(1024)} all-reduce(f32[5632]{0:T(1024)} %convert_reduce_fusion), channel_id=3, replica_groups=mesh['groups'=2,'fsdp'=8,'band'=2] {'fsdp'}, use_global_device_ids=true, to_apply=%region_4.5.clone | all-reduce | flops 5632 | bytes 45056
  208.8 0.8 dynamic-slice.2
  209.6 1.8 copy.80
  211.4 11.0 %all-reduce.4 = (f32[9,704]{1,0:T(8,128)}, f32[704]{0:T(1024)}) all-reduce(f32[9,704]{1,0:T(8,128)} %copy.80, f32[704]{0:T(1024)S(1)} %dynamic-slice.2), channel_id=1, replica_groups=mesh['groups'=2,'fsdp'=8,'band'=2] {'band'}, use_global_device_ids=true, to_apply=%region_0.1 | all-reduce | flops 7040 | bytes 56320 | tf_op jit(solution)/shard_map/psum | solution.py:77
  222.4 1.8 select_maximum_fusion
  224.2 4.5 %fusion.12 = bf16[1,2,64,5632]{3,2,1,0:T(8,128)(2,1)} fusion(bf16[1,4,66,5632]{3,2,1,0:T(8,128)(2,1)S(1)} %select_maximum_fusion, bf16[1,1,64,5632]{3,2,1,0:T(8,128)(2,1)S(1)} %collective-permute-done.2, bf16[1,2,64,2816]{3,2,1,0:T(8,128)(2,1)S(1)} %get-tuple-element.28, bf16[1,2,64,2816]{3,2,1,0:T(8,128)(2,1)S(1)} %get-tuple-element.29, ...), kind=kLoop, calls=%fused_computation.29 | loop fusion | flops 28835840 | bytes 13178880 | tf_op jit(solution)/shard_map/convert_element_type | solution.py:74
  (49 shorter events, 0.1 us)
Async XLA Ops:
  7.2 127.2 %copy-start = (bf16[1,2,64,2240]{3,2,1,0:T(8,128)(2,1)S(1)}, bf16[1,2,64,2240]{3,2,1,0:T(8,128)(2,1)}, u32[]{:S(2)}) copy-start(bf16[1,2,64,2240]{3,2,1,0:T(8,128)(2,1)} %param.9) | copy-start | bytes 1720324
  7.2 9.7 %copy-start.22 = (u32[32]{0:T(128)S(1)}, u32[32]{0:T(128)}, u32[]{:S(2)}) copy-start(u32[32]{0:T(128)} %constant.15) | copy-start | bytes 388
  7.2 73.9 %copy-start.3 = (bf16[1,2,64,5632]{3,2,1,0:T(8,128)(2,1)S(1)}, bf16[1,2,64,5632]{3,2,1,0:T(8,128)(2,1)}, u32[]{:S(2)}) copy-start(bf16[1,2,64,5632]{3,2,1,0:T(8,128)(2,1)} %param.5) | copy-start | bytes 4325380
  7.2 10.9 %copy-start.23 = (bf16[704]{0:T(1024)(128)(2,1)S(1)}, bf16[704]{0:T(1024)(128)(2,1)}, u32[]{:S(2)}) copy-start(bf16[704]{0:T(1024)(128)(2,1)} %param.7) | copy-start | bytes 4228
  7.2 43.2 %copy-start.21 = (bf16[9,704]{1,0:T(8,128)(2,1)S(1)}, bf16[9,704]{1,0:T(8,128)(2,1)}, u32[]{:S(2)}) copy-start(bf16[9,704]{1,0:T(8,128)(2,1)} %param.6) | copy-start | bytes 38020
  7.2 127.1 %all-gather.3.cloned.1.call-start = ((), (), s32[]{:S(2)}) async-start(), calls=%async_computation.1 | async-start | bytes 14598144 | tf_op jit(solution)/shard_map/all_gather | solution.py:48
  8.0 201.7 %reduce-scatter.4.cloned.1.call-start = ((), (), s32[]{:S(2)}) async-start(), calls=%async_computation.2 | async-start | bytes 3244032
  10.6 70.5 %collective-permute-start.1 = (bf16[1,1,64,5632]{3,2,1,0:T(8,128)(2,1)}, bf16[1,1,64,5632]{3,2,1,0:T(8,128)(2,1)S(1)}, u32[]{:S(2)}, u32[]{:S(2)}) collective-permute-start(bf16[1,1,64,5632]{3,2,1,0:T(8,128)(2,1)} %get-tuple-element.39), channel_id=1, source_target_pairs={{1,0},{3,2},{5,4},{7,6},{9,8},{11,10},{13,12},{15,14},{17,16},{19,... | collective-permute-start | bytes 2162696 | tf_op jit(solution)/shard_map/ppermute | solution.py:17
  11.9 69.3 %collective-permute-start = (bf16[1,1,64,5632]{3,2,1,0:T(8,128)(2,1)}, bf16[1,1,64,5632]{3,2,1,0:T(8,128)(2,1)S(1)}, u32[]{:S(2)}, u32[]{:S(2)}) collective-permute-start(bf16[1,1,64,5632]{3,2,1,0:T(8,128)(2,1)} %get-tuple-element.40), channel_id=1, source_target_pairs={{0,1},{2,3},{4,5},{6,7},{8,9},{10,11},{12,13},{14,15},{16,17},{18,... | collective-permute-start | bytes 2162696 | tf_op jit(solution)/shard_map/ppermute | solution.py:15
  81.0 1.2 copy-start.8
  81.0 1.2 copy-start.10
  81.1 1.2 copy-start.12
  81.1 1.2 copy-start.14
  81.1 1.2 copy-start.16
  81.1 1.2 copy-start.18
  81.1 2.8 %copy-start.20 = (f32[5632]{0:T(1024)S(1)}, f32[5632]{0:T(1024)}, u32[]{:S(2)}) copy-start(f32[5632]{0:T(1024)} %convert_element_type.109) | copy-start | bytes 67588
  81.1 1.2 copy-start.4
  81.2 1.2 copy-start.6
  82.2 1.7 copy-start.1
  134.3 12.0 %copy-start.2 = (bf16[1,4,66,5632]{3,2,1,0:T(8,128)(2,1)S(1)}, bf16[1,4,66,5632]{3,2,1,0:T(8,128)(2,1)}, u32[]{:S(2)}) copy-start(bf16[1,4,66,5632]{3,2,1,0:T(8,128)(2,1)} %copy-done.1) | copy-start | bytes 8921092
  145.1 1.4 copy-start.5
  145.1 1.8 copy-start.7
  156.4 66.0 %collective-permute-start.2 = (bf16[1,1,64,5632]{3,2,1,0:T(8,128)(2,1)}, bf16[1,1,64,5632]{3,2,1,0:T(8,128)(2,1)S(1)}, u32[]{:S(2)}, u32[]{:S(2)}) collective-permute-start(bf16[1,1,64,5632]{3,2,1,0:T(8,128)(2,1)} %get-tuple-element.37), channel_id=1, source_target_pairs={{0,1},{2,3},{4,5},{6,7},{8,9},{10,11},{12,13},{14,15},{16,17},{18,... | collective-permute-start | bytes 2162696 | tf_op jit(solution)/shard_map/ppermute | solution.py:15
  159.7 62.7 %collective-permute-start.3 = (bf16[1,1,64,5632]{3,2,1,0:T(8,128)(2,1)}, bf16[1,1,64,5632]{3,2,1,0:T(8,128)(2,1)S(1)}, u32[]{:S(2)}, u32[]{:S(2)}) collective-permute-start(bf16[1,1,64,5632]{3,2,1,0:T(8,128)(2,1)} %get-tuple-element.38), channel_id=1, source_target_pairs={{1,0},{3,2},{5,4},{7,6},{9,8},{11,10},{13,12},{15,14},{17,16},{19,... | collective-permute-start | bytes 2162696 | tf_op jit(solution)/shard_map/ppermute | solution.py:17
  222.3 1.8 copy-start.9
  222.3 1.8 copy-start.11
  222.3 1.8 copy-start.13
  222.3 1.8 copy-start.15
  222.3 1.8 copy-start.17
  222.4 1.8 copy-start.19
Sparse Core Ops, SparseCore 0:
  9.7 124.6 all-gather.2
  167.5 38.8 reduce-scatter.3
where the time goes:
time: 236 us
  blocking collectives  95.2 us (40%)
  waiting for transfers between devices  47.2 us (20%)
  local copies, waits for them, and re-layouts  26.3 us (11%)
  matrix products  21.6 us (9%)
  other arithmetic  18.4 us (8%)
  between operations  15.7 us (7%)
  starting transfers between devices  11.1 us (5%)
    unnamed x2, blocking collectives  59.2 us
    all_gather x1, waiting for transfers between devices, body(): piece = lax.all_gather(w_out, 'fsdp', axis=0, tiled=True)  46.5 us
    all_gather x1, blocking collectives, body(): lax.all_gather(tap_weights, 'fsdp', axis=1, tiled=True)  25 us
    psum x1, blocking collectives, body(): tap_grad, bias_grad = lax.psum((tap_grad, bias_grad), 'band')  11 us
    dot_general x1, matrix products, body(): out_sum = jnp.dot(glu_flat, piece, preferred_element_type=jnp.float32)  10.8 us
    dot_general x1, matrix products, body(): lax.dot_general(grad_flat, piece, (((1,), (1,)), ((), ())), preferred_ele...  10.8 us
    another operation x10, local copies, waits for them, and re-layouts, body(): tap_grad = jnp.stack(tap_terms)  8.77 us
    unnamed x54, local copies, waits for them, and re-layouts  8.64 us
  transfers between devices with their start and end apart: 6, of which 1 were waited for; matrix products, arithmetic and copies ran while one was open for 15% of the time, Pallas kernels for 0%

commit v1 on v0

--- a/solution.py
+++ b/solution.py
@@ -45,7 +45,14 @@
     glu_flat = (values_half * silu_gate).astype(jnp.bfloat16).reshape(token_count, hidden_units)
     grad_flat = cotangent.reshape(token_count, cotangent.shape[3])
     features = grad_flat.shape[1]
-    piece = lax.all_gather(w_out, "fsdp", axis=0, tiled=True)
+    ways, here = (lax.axis_size("fsdp"), lax.axis_index("fsdp"))
+    piece, reach = (w_out, 1)
+    while reach < ways:
+        theirs = lax.ppermute(piece, "fsdp", [(d, d ^ reach) for d in range(ways)])
+        mine_first = jnp.concatenate([piece, theirs], axis=0)
+        theirs_first = jnp.concatenate([theirs, piece], axis=0)
+        piece = jnp.where(here & reach == 0, mine_first, theirs_first)
+        reach = 2 * reach
     out_sum = jnp.dot(glu_flat, piece, preferred_element_type=jnp.float32)
     d_piece = lax.dot_general(
         grad_flat, piece, (((1,), (1,)), ((), ())), preferred_element_type=jnp.float32

time: 236 us -> 534 us (2.26)
  blocking collectives: 95.2 us -> 334 us
  waiting for transfers between devices: 47.2 us -> 74.2 us
  other arithmetic: 18.4 us -> 35 us
  starting transfers between devices: 11.1 us -> 18.7 us
    all_gather x1, blocking collectives: 25 us -> 274 us  [body(): lax.all_gather(tap_weights, 'fsdp', axis=1, tiled=True)]
    ppermute x0 -> x3, waiting for transfers between devices: none -> 74.1 us  [body(): theirs = lax.ppermute(piece, 'fsdp', [(d, d ^ reach) for d in range(ways)])]
    all_gather x1 -> x0, waiting for transfers between devices: 46.5 us -> none  [body(): piece = lax.all_gather(w_out, 'fsdp', axis=0, tiled=True)]
    select_n x0 -> x2, other arithmetic: none -> 13.2 us  [body(): piece = jnp.where(here & reach == 0, mine_first, theirs_first)]
    select_n x0 -> x1, local copies, waits for them, and re-layouts: none -> 9.47 us  [body(): piece = jnp.where(here & reach == 0, mine_first, theirs_first)]
    ppermute x0 -> x1, local copies, waits for them, and re-layouts: none -> 9.31 us  [body(): theirs = lax.ppermute(piece, 'fsdp', [(d, d ^ reach) for d in range(ways)])]
    another operation x10, local copies, waits for them, and re-layouts: 8.77 us -> 0.46 us  [body(): tap_grad = jnp.stack(tap_terms)]
    unnamed x2, blocking collectives: 59.2 us -> 52.4 us
  transfers between devices with their start and end apart: 6 -> 8, of which waited for: 1 -> 2; matrix products, arithmetic and copies ran while one was open for 15% -> 7% of each run, Pallas kernels for 0% -> 0%
where the time goes in v1:
time: 534 us
  blocking collectives  334 us (63%)
  waiting for transfers between devices  74.2 us (14%)
  other arithmetic  35 us (7%)
  local copies, waits for them, and re-layouts  31.3 us (6%)
  matrix products  24.7 us (5%)
  starting transfers between devices  18.7 us (4%)
  between operations  15.8 us (3%)
    all_gather x1, blocking collectives, body(): lax.all_gather(tap_weights, 'fsdp', axis=1, tiled=True)  274 us
    ppermute x3, waiting for transfers between devices, body(): theirs = lax.ppermute(piece, 'fsdp', [(d, d ^ reach) for d in range(ways)])  74.1 us
    unnamed x2, blocking collectives  52.4 us
    select_n x2, other arithmetic, body(): piece = jnp.where(here & reach == 0, mine_first, theirs_first)  13.2 us
    dot_general x1, matrix products, body(): out_sum = jnp.dot(glu_flat, piece, preferred_element_type=jnp.float32)  13 us
    dot_general x1, matrix products, body(): lax.dot_general(grad_flat, piece, (((1,), (1,)), ((), ())), preferred_ele...  11.7 us
  transfers between devices with their start and end apart: 8, of which 2 were waited for; matrix products, arithmetic and copies ran while one was open for 7% of the time, Pallas kernels for 0%

profile of v1, /device:TPU:0, one launch (start us, length us, event | category | flops | bytes accessed | tf_op | source)
XLA Modules:
  0.0 533.6 jit_solution(10792565081676744686)
XLA Ops:
  7.2 0.0 copy-start
  7.2 0.0 reduce-scatter.4.cloned.1.call-start
  7.2 0.6 collective-permute-start.2
  7.8 3.3 collective-permute-done.2
  11.1 4.0 maximum_select_fusion.2
  15.1 2.9 collective-permute-start.3
  18.0 70.8 %collective-permute-done.3 = bf16[704,2240]{1,0:T(8,128)(2,1)} collective-permute-done((bf16[704,2240]{1,0:T(8,128)(2,1)}, bf16[704,2240]{1,0:T(8,128)(2,1)}, u32[]{:S(2)}, u32[]{:S(2)}) %collective-permute-start.3) | collective-permute-done | bytes 3153952 | tf_op jit(solution)/shard_map/ppermute | solution.py:51
  88.8 9.2 %maximum_select_fusion.1 = bf16[1408,2240]{1,0:T(8,128)(2,1)} fusion(bf16[704,2240]{1,0:T(8,128)(2,1)} %collective-permute-done.3, bf16[704,2240]{1,0:T(8,128)(2,1)} %maximum_select_fusion.2, pred[]{:T(512)S(6)} %eq.10), kind=kLoop, calls=%fused_computation.12 | loop fusion | flops 28385280 | bytes 12615681 | tf_op jit(solution)/shard_map/jit(_where)/select_n | solution.py:54
  98.0 9.5 %copy.23 = bf16[1408,2240]{0,1:T(8,128)(2,1)} copy(bf16[1408,2240]{1,0:T(8,128)(2,1)} %maximum_select_fusion.1) | data formatting | bytes 12615680 | tf_op jit(solution)/shard_map/jit(_where)/select_n | solution.py:54
  107.5 2.8 collective-permute-start.4
  110.3 1.2 fusion.23
  111.5 3.4 collective-permute-start
  115.0 1.3 collective-permute-start.1
  116.3 273.7 %all-gather = bf16[8,704,9]{1,2,0:T(8,128)(2,1)S(1)} all-gather(bf16[1,704,9]{1,2,0:T(8,128)(2,1)S(1)} %bitcast.93), channel_id=1, replica_groups=mesh['groups'=2,'fsdp'=8,'band'=2] {'fsdp'}, dimensions={0}, use_global_device_ids=true | all-gather | bytes 114048 | tf_op jit(solution)/shard_map/all_gather | solution.py:26
  390.0 0.7 copy_convert_fusion
  390.7 1.8 reshape.189
  392.5 0.6 fusion.24
  393.8 0.2 dynamic-update-slice
  394.0 26.2 %all-reduce.2 = bf16[5632]{0:T(1024)(128)(2,1)S(1)} all-reduce(bf16[5632]{0:T(1024)(128)(2,1)S(1)} %dynamic-update-slice), channel_id=1, replica_groups=mesh['groups'=2,'fsdp'=8,'band'=2] {'fsdp'}, use_global_device_ids=true, to_apply=%add.2 | all-reduce | flops 5632 | bytes 22528
  420.2 0.6 convert_element_type.109
  421.5 2.7 slice_reduce_fusion.8
  424.3 0.0 copy-start.22
  424.3 0.0 collective-permute-done
  424.3 0.0 collective-permute-done.1
  424.3 1.1 select_maximum_fusion.3
  425.5 4.0 multiply_add_fusion
  429.5 9.3 %copy.24 = bf16[1408,2240]{1,0:T(8,128)(2,1)} copy(bf16[1408,2240]{0,1:T(8,128)(2,1)} %collective-permute-done.4) | data formatting | bytes 12615680 | tf_op jit(solution)/shard_map/ppermute | solution.py:51
  438.8 11.7 %fusion.17 = f32[2816,128]{0,1:T(8,128)S(1)} fusion(bf16[128,2240]{1,0:T(8,128)(2,1)S(1)} %bitcast.84, bf16[1408,2240]{1,0:T(8,128)(2,1)} %copy.24, bf16[1408,2240]{1,0:T(8,128)(2,1)} %maximum_select_fusion.1, pred[]{:T(512)S(6)} %eq.9), kind=kOutput, calls=%fused_computation.40 | convolution fusion | flops 1671577600 | bytes 14630913 | tf_op jit(solution)/shard_map/dot_general | solution.py:57
  450.5 1.7 multiply_convert_fusion
  452.1 1.2 fusion.19
  453.3 1.3 collective-permute-start.6
  454.6 6.3 %collective-permute-start.5 = (bf16[1,1,64,5632]{3,2,1,0:T(8,128)(2,1)}, bf16[1,1,64,5632]{3,2,1,0:T(8,128)(2,1)}, u32[]{:S(2)}, u32[]{:S(2)}) collective-permute-start(bf16[1,1,64,5632]{3,2,1,0:T(8,128)(2,1)} %get-tuple-element.37), channel_id=1, source_target_pairs={{0,1},{2,3},{4,5},{6,7},{8,9},{10,11},{12,13},{14,15},{16,17},{18,... | collective-permute-start | bytes 2162696 | tf_op jit(solution)/shard_map/ppermute | solution.py:15
  460.9 3.8 fusion.14
  465.0 0.3 stack.39
  465.3 0.0 copy-start.9
  465.3 2.1 copy.90
  467.4 0.0 reduce-scatter.4.cloned.1.call-update
  467.5 13.0 %convolution_convert_fusion = bf16[128,2240]{0,1:T(8,128)(2,1)} fusion(bf16[128,2816]{1,0:T(8,128)(2,1)S(1)} %bitcast.90, bf16[1408,2240]{1,0:T(8,128)(2,1)} %copy.24, bf16[1408,2240]{1,0:T(8,128)(2,1)} %maximum_select_fusion.1, pred[]{:T(512)S(6)} %eq.9), kind=kOutput, calls=%fused_computation.14 | convolution fusion | flops 1671864320 | bytes 13910017 | tf_op jit(solution)/shard_map/dot_general | solution.py:56
  480.5 2.1 copy.26
  482.6 0.2 convert_reduce_fusion
  482.8 26.2 %all-reduce.3 = f32[5632]{0:T(1024)S(1)} all-reduce(f32[5632]{0:T(1024)S(1)} %convert_reduce_fusion), channel_id=3, replica_groups=mesh['groups'=2,'fsdp'=8,'band'=2] {'fsdp'}, use_global_device_ids=true, to_apply=%region_4.5.clone | all-reduce | flops 5632 | bytes 45056
  509.0 0.1 dynamic-slice.2
  509.1 1.1 copy.91
  510.2 7.8 %all-reduce.4 = (f32[9,704]{1,0:T(8,128)}, f32[704]{0:T(1024)}) all-reduce(f32[9,704]{1,0:T(8,128)S(1)} %copy.91, f32[704]{0:T(1024)S(1)} %dynamic-slice.2), channel_id=1, replica_groups=mesh['groups'=2,'fsdp'=8,'band'=2] {'band'}, use_global_device_ids=true, to_apply=%region_0.1 | all-reduce | flops 7040 | bytes 56320 | tf_op jit(solution)/shard_map/psum | solution.py:84
  518.1 0.0 collective-permute-done.6
  518.1 0.0 collective-permute-done.5
  518.1 2.9 select_maximum_fusion
  521.0 5.7 %fusion.7 = bf16[1,2,64,5632]{3,2,1,0:T(8,128)(2,1)} fusion(bf16[1,4,66,5632]{3,2,1,0:T(8,128)(2,1)S(1)} %select_maximum_fusion, bf16[1,1,64,5632]{3,2,1,0:T(8,128)(2,1)} %collective-permute-done.5, bf16[1,2,64,2816]{3,2,1,0:T(8,128)(2,1)S(1)} %get-tuple-element.28, bf16[1,2,64,2816]{3,2,1,0:T(8,128)(2,1)S(1)} %get-tuple-element.29, ...), kind=kLoop, calls=%fused_computation.29 | loop fusion | flops 28835840 | bytes 13178880 | tf_op jit(solution)/shard_map/convert_element_type | solution.py:81
  (61 shorter events, 0.3 us)
Async XLA Ops:
  7.2 431.6 %copy-start = (bf16[1,2,64,2240]{3,2,1,0:T(8,128)(2,1)S(1)}, bf16[1,2,64,2240]{3,2,1,0:T(8,128)(2,1)}, u32[]{:S(2)}) copy-start(bf16[1,2,64,2240]{3,2,1,0:T(8,128)(2,1)} %param.9) | copy-start | bytes 1720324
  7.2 501.9 %reduce-scatter.4.cloned.1.call-start = ((), (), s32[]{:S(2)}) async-start(), calls=%async_computation.1 | async-start | bytes 3244032
  7.2 3.9 collective-permute-start.2
  15.1 73.8 %collective-permute-start.3 = (bf16[704,2240]{1,0:T(8,128)(2,1)}, bf16[704,2240]{1,0:T(8,128)(2,1)}, u32[]{:S(2)}, u32[]{:S(2)}) collective-permute-start(bf16[704,2240]{1,0:T(8,128)(2,1)} %maximum_select_fusion.2), channel_id=1, source_target_pairs={{0,4},{2,6},{4,0},{6,2},{8,12},{10,14},{12,8},{14,10},{1,5},{3,7},... | collective-permute-start | bytes 9461768 | tf_op jit(solution)/shard_map/ppermute | solution.py:51
  98.0 12.3 %copy-start.3 = (bf16[1,2,64,5632]{3,2,1,0:T(8,128)(2,1)S(1)}, bf16[1,2,64,5632]{3,2,1,0:T(8,128)(2,1)}, u32[]{:S(2)}) copy-start(bf16[1,2,64,5632]{3,2,1,0:T(8,128)(2,1)} %param.5) | copy-start | bytes 4325380
  107.5 8.8 %copy-start.23 = (bf16[9,704]{1,0:T(8,128)(2,1)S(1)}, bf16[9,704]{1,0:T(8,128)(2,1)}, u32[]{:S(2)}) copy-start(bf16[9,704]{1,0:T(8,128)(2,1)} %param.6) | copy-start | bytes 38020
  107.5 285.0 %copy-start.24 = (u32[32]{0:T(128)S(1)}, u32[32]{0:T(128)}, u32[]{:S(2)}) copy-start(u32[32]{0:T(128)} %constant.28) | copy-start | bytes 388
  107.5 286.3 %copy-start.25 = (bf16[704]{0:T(1024)(128)(2,1)S(1)}, bf16[704]{0:T(1024)(128)(2,1)}, u32[]{:S(2)}) copy-start(bf16[704]{0:T(1024)(128)(2,1)} %param.7) | copy-start | bytes 4228
  107.5 321.9 %collective-permute-start.4 = (bf16[1408,2240]{0,1:T(8,128)(2,1)}, bf16[1408,2240]{0,1:T(8,128)(2,1)}, u32[]{:S(2)}, u32[]{:S(2)}) collective-permute-start(bf16[1408,2240]{0,1:T(8,128)(2,1)} %copy.23), channel_id=1, source_target_pairs={{0,8},{2,10},{4,12},{6,14},{8,0},{10,2},{12,4},{14,6},{1,9},{3,11}... | collective-permute-start | bytes 18923528 | tf_op jit(solution)/shard_map/ppermute | solution.py:51
  111.5 312.7 %collective-permute-start = (bf16[1,1,64,5632]{3,2,1,0:T(8,128)(2,1)}, bf16[1,1,64,5632]{3,2,1,0:T(8,128)(2,1)S(1)}, u32[]{:S(2)}, u32[]{:S(2)}) collective-permute-start(bf16[1,1,64,5632]{3,2,1,0:T(8,128)(2,1)} %get-tuple-element.40), channel_id=1, source_target_pairs={{0,1},{2,3},{4,5},{6,7},{8,9},{10,11},{12,13},{14,15},{16,17},{18,... | collective-permute-start | bytes 2162696 | tf_op jit(solution)/shard_map/ppermute | solution.py:15
  115.0 309.3 %collective-permute-start.1 = (bf16[1,1,64,5632]{3,2,1,0:T(8,128)(2,1)}, bf16[1,1,64,5632]{3,2,1,0:T(8,128)(2,1)S(1)}, u32[]{:S(2)}, u32[]{:S(2)}) collective-permute-start(bf16[1,1,64,5632]{3,2,1,0:T(8,128)(2,1)} %get-tuple-element.39), channel_id=1, source_target_pairs={{1,0},{3,2},{5,4},{7,6},{9,8},{11,10},{13,12},{15,14},{17,16},{19,... | collective-permute-start | bytes 2162696 | tf_op jit(solution)/shard_map/ppermute | solution.py:17
  424.2 1.2 copy-start.10
  424.2 1.2 copy-start.12
  424.2 1.2 copy-start.14
  424.2 1.2 copy-start.16
  424.2 1.2 copy-start.18
  424.2 1.2 copy-start.20
  424.3 1.2 copy-start.22
  424.3 1.2 copy-start.5
  424.3 1.2 copy-start.7
  425.4 4.1 copy-start.1
  438.8 11.7 %copy-start.4 = (f32[1,2,64,5632]{3,2,1,0:T(8,128)S(1)}, f32[1,2,64,5632]{3,2,1,0:T(8,128)}, u32[]{:S(2)}) copy-start(f32[1,2,64,5632]{3,2,1,0:T(8,128)} %multiply_add_fusion) | copy-start | bytes 8650756
  450.5 10.5 %copy-start.2 = (bf16[1,4,66,5632]{3,2,1,0:T(8,128)(2,1)S(1)}, bf16[1,4,66,5632]{3,2,1,0:T(8,128)(2,1)}, u32[]{:S(2)}) copy-start(bf16[1,4,66,5632]{3,2,1,0:T(8,128)(2,1)} %copy-done.1) | copy-start | bytes 8921092
  452.1 8.8 %copy-start.6 = (bf16[1,1,64,5632]{3,2,1,0:T(8,128)(2,1)S(1)}, bf16[1,1,64,5632]{3,2,1,0:T(8,128)(2,1)}, u32[]{:S(2)}) copy-start(bf16[1,1,64,5632]{3,2,1,0:T(8,128)(2,1)} %copy-done.5) | copy-start | bytes 2162692
  452.1 8.8 %copy-start.8 = (bf16[1,1,64,5632]{3,2,1,0:T(8,128)(2,1)S(1)}, bf16[1,1,64,5632]{3,2,1,0:T(8,128)(2,1)}, u32[]{:S(2)}) copy-start(bf16[1,1,64,5632]{3,2,1,0:T(8,128)(2,1)} %copy-done.7) | copy-start | bytes 2162692
  453.3 64.7 %collective-permute-start.6 = (bf16[1,1,64,5632]{3,2,1,0:T(8,128)(2,1)}, bf16[1,1,64,5632]{3,2,1,0:T(8,128)(2,1)}, u32[]{:S(2)}, u32[]{:S(2)}) collective-permute-start(bf16[1,1,64,5632]{3,2,1,0:T(8,128)(2,1)} %get-tuple-element.38), channel_id=1, source_target_pairs={{1,0},{3,2},{5,4},{7,6},{9,8},{11,10},{13,12},{15,14},{17,16},{19,... | collective-permute-start | bytes 2162696 | tf_op jit(solution)/shard_map/ppermute | solution.py:17
  454.6 63.5 %collective-permute-start.5 = (bf16[1,1,64,5632]{3,2,1,0:T(8,128)(2,1)}, bf16[1,1,64,5632]{3,2,1,0:T(8,128)(2,1)}, u32[]{:S(2)}, u32[]{:S(2)}) collective-permute-start(bf16[1,1,64,5632]{3,2,1,0:T(8,128)(2,1)} %get-tuple-element.37), channel_id=1, source_target_pairs={{0,1},{2,3},{4,5},{6,7},{8,9},{10,11},{12,13},{14,15},{16,17},{18,... | collective-permute-start | bytes 2162696 | tf_op jit(solution)/shard_map/ppermute | solution.py:15
  465.3 2.1 copy-start.9
  518.0 2.9 copy-start.11
  518.0 2.9 copy-start.13
  518.1 2.9 copy-start.15
  518.1 3.0 copy-start.17
  518.1 3.0 copy-start.19
  518.1 3.0 copy-start.21
Sparse Core Ops, SparseCore 0:
  467.6 36.4 reduce-scatter.3
